TPU v7x, 32 devices: a whole 2x2x4 slice. The times are simulated.
32 devices in a mesh: dp: 4 (over z), ctx: 8 (over y, x, core).
Axes of the slice: x: 2, y: 2, z: 4, core: 2. Of those that a mesh axis runs over, the one named last changes fastest.
Arguments:
- queries: bfloat16 [4, 4096, 1024], P('dp', 'ctx'), may hold values from -6 to 6
- key_vectors: bfloat16 [4, 4096, 1024], P('dp', 'ctx'), may hold values from -6 to 6
- value_vectors: bfloat16 [4, 4096, 1024], P('dp', 'ctx'), may hold values from -6 to 6
- out_grad: bfloat16 [4, 4096, 1024], P('dp', 'ctx'), may hold values from -6 to 6
- column_bias: float32 [8], replicated, may hold values from -1 to 2
- column_offsets: int32 [1], replicated, may hold values from 0 to 63
Outputs:
- attended: bfloat16 [4, 4096, 1024], P('dp', 'ctx')
- query_grad: bfloat16 [4, 4096, 1024], P('dp', 'ctx')
- key_grad: bfloat16 [4, 4096, 1024], P('dp', 'ctx')
- value_grad: bfloat16 [4, 4096, 1024], P('dp', 'ctx')
- bias_grad: float32 [8], replicated
All inputs are finite; a program needn't handle non-finite values.
Results may differ from a plain program's by a relative error of at most 0.005.
The roundings to bfloat16 on the way count: a program that leaves them out, or rounds other values in their place, can miss the bound.
Values may be sent and summed in bfloat16 or wider, within the bound.
A program may use at most 128 MiB of HBM per device.

v0:
```python
import jax
import jax.numpy as jnp
from jax import lax
from jax.sharding import PartitionSpec as P

HEADS = 8
HEAD_DIM = 128
LOCAL_BAND = 512
STRIDE = 4096
CB = 64
TOKENS_PER_SHARD = 512


def from_behind(value, axis, by):
    size = lax.axis_size(axis)
    pairs = [(i, i + by) for i in range(size) if 0 <= i + by < size]
    return lax.ppermute(value, axis, pairs)


def column_flags(positions, offsets):
    window = positions // STRIDE
    within = positions % STRIDE
    picks = window[:, None] == jnp.arange(offsets.shape[0], dtype=jnp.int32)[None, :]
    offset_at = jnp.sum(jnp.where(picks, offsets[None, :], 0), axis=1)
    return (positions >= 0) & (within // CB == offset_at)


def head_block(qh, kb, vb, kc, vc, doh, bias_h, band_ok, band_col, col_ok):
    scale = HEAD_DIM ** (-0.5)
    sb = (
        jnp.dot(qh, kb.T, preferred_element_type=jnp.float32) * scale
        + jnp.where(band_col, bias_h, 0.0)[None, :]
    )
    sc = jnp.dot(qh, kc.T, preferred_element_type=jnp.float32) * scale + bias_h
    sb = jnp.where(band_ok, sb, -jnp.inf)
    sc = jnp.where(col_ok, sc, -jnp.inf)
    top = jnp.maximum(jnp.max(sb, axis=1), jnp.max(sc, axis=1))
    pb = jnp.exp(sb - top[:, None])
    pc = jnp.exp(sc - top[:, None])
    total = jnp.sum(pb, axis=1) + jnp.sum(pc, axis=1)
    wb = pb / total[:, None]
    wc = pc / total[:, None]
    wb16 = wb.astype(jnp.bfloat16)
    wc16 = wc.astype(jnp.bfloat16)
    mixed = jnp.dot(wb16, vb, preferred_element_type=jnp.float32) + jnp.dot(
        wc16, vc, preferred_element_type=jnp.float32
    )
    oh = mixed.astype(jnp.bfloat16)
    delta = jnp.sum(doh.astype(jnp.float32) * oh.astype(jnp.float32), axis=1)
    dsb = wb * (jnp.dot(doh, vb.T, preferred_element_type=jnp.float32) - delta[:, None])
    dsc = wc * (jnp.dot(doh, vc.T, preferred_element_type=jnp.float32) - delta[:, None])
    dbias = jnp.sum(jnp.where(band_col[None, :], dsb, 0.0)) + jnp.sum(dsc)
    dsb16 = dsb.astype(jnp.bfloat16)
    dsc16 = dsc.astype(jnp.bfloat16)
    dq = (
        (
            jnp.dot(dsb16, kb, preferred_element_type=jnp.float32)
            + jnp.dot(dsc16, kc, preferred_element_type=jnp.float32)
        )
        * scale
    ).astype(jnp.bfloat16)
    dkb = jnp.dot(dsb16.T, qh, preferred_element_type=jnp.float32) * scale
    dvb = jnp.dot(wb16.T, doh, preferred_element_type=jnp.float32)
    dkc = jnp.dot(dsc16.T, qh, preferred_element_type=jnp.float32) * scale
    dvc = jnp.dot(wc16.T, doh, preferred_element_type=jnp.float32)
    return (oh, dq, dkb, dvb, dkc, dvc, dbias, top, total, delta)


def separate_heads(x):
    return x.reshape(x.shape[0], HEADS, HEAD_DIM).transpose(1, 0, 2)


def join_heads(x):
    return x.transpose(1, 0, 2).reshape(x.shape[1], HEADS * HEAD_DIM)


def per_device(queries, key_vectors, value_vectors, out_grad, column_bias, column_offsets):
    here = lax.axis_index("ctx")
    count = lax.axis_size("ctx")
    start_position = here * TOKENS_PER_SHARD
    width = queries.shape[2]
    query_rows = queries[0]
    key_rows = key_vectors[0]
    value_rows = value_vectors[0]
    grad_rows = out_grad[0]
    ncol = column_offsets.shape[0]
    block_starts = jnp.arange(ncol, dtype=jnp.int32) * STRIDE + column_offsets * CB
    colpos = jnp.repeat(block_starts, CB) + jnp.tile(jnp.arange(CB, dtype=jnp.int32), ncol)
    window = start_position // STRIDE
    own_start = window * STRIDE + column_offsets[window] * CB
    local = jnp.clip(own_start - start_position, 0, TOKENS_PER_SHARD - CB)
    piece_k = lax.dynamic_slice_in_dim(key_rows, local, CB, 0)
    piece_v = lax.dynamic_slice_in_dim(value_rows, local, CB, 0)
    pieces_k, pieces_v = (
        lax.all_gather(piece_k, "ctx", axis=0, tiled=True),
        lax.all_gather(piece_v, "ctx", axis=0, tiled=True),
    )
    owner = block_starts // TOKENS_PER_SHARD
    col_k = pieces_k.reshape(count, CB, width)[owner].reshape(ncol * CB, width)
    col_v = pieces_v.reshape(count, CB, width)[owner].reshape(ncol * CB, width)
    prev_k, prev_v = from_behind((key_rows, value_rows), "ctx", 1)
    band_k = jnp.concatenate([prev_k, key_rows], axis=0)
    band_v = jnp.concatenate([prev_v, value_rows], axis=0)
    qpos = start_position + jnp.arange(TOKENS_PER_SHARD, dtype=jnp.int32)
    kpos = start_position - LOCAL_BAND + jnp.arange(LOCAL_BAND + TOKENS_PER_SHARD, dtype=jnp.int32)
    gap = qpos[:, None] - kpos[None, :]
    band_ok = (kpos[None, :] >= 0) & (gap >= 0) & (gap < LOCAL_BAND)
    band_col = column_flags(kpos, column_offsets)
    col_ok = colpos[None, :] <= qpos[:, None] - LOCAL_BAND

    def per_head(items):
        return head_block(
            items[0],
            items[1],
            items[2],
            items[3],
            items[4],
            items[5],
            items[6],
            band_ok,
            band_col,
            col_ok,
        )

    results = lax.map(
        per_head,
        (
            separate_heads(query_rows),
            separate_heads(band_k),
            separate_heads(band_v),
            separate_heads(col_k),
            separate_heads(col_v),
            separate_heads(grad_rows),
            column_bias,
        ),
    )
    oh, dq, dkb, dvb, dkc, dvc, dbias, top, total, delta = results
    attended = join_heads(oh)
    query_grad = join_heads(dq)
    dk_band = join_heads(dkb)
    dv_band = join_heads(dvb)
    own_dk = dk_band[dk_band.shape[0] - TOKENS_PER_SHARD :]
    own_dv = dv_band[dv_band.shape[0] - TOKENS_PER_SHARD :]
    back_k, back_v = from_behind((dk_band[:LOCAL_BAND], dv_band[:LOCAL_BAND]), "ctx", -1)
    own_dk = own_dk.at[TOKENS_PER_SHARD - LOCAL_BAND :].add(back_k)
    own_dv = own_dv.at[TOKENS_PER_SHARD - LOCAL_BAND :].add(back_v)
    summed_k, summed_v = lax.psum((join_heads(dkc), join_heads(dvc)), "ctx")
    flags = column_flags(qpos, column_offsets)
    source = jnp.clip(qpos // STRIDE * CB + qpos % CB, 0, ncol * CB - 1)
    own_dk = own_dk + jnp.where(flags[:, None], summed_k[source], 0.0)
    own_dv = own_dv + jnp.where(flags[:, None], summed_v[source], 0.0)
    bias_grad = lax.psum(dbias, ("dp", "ctx"))
    return (
        attended[None],
        query_grad[None],
        own_dk.astype(jnp.bfloat16)[None],
        own_dv.astype(jnp.bfloat16)[None],
        bias_grad,
    )


def solution(mesh):
    placed = (
        P("dp", "ctx", None),
        P("dp", "ctx", None),
        P("dp", "ctx", None),
        P("dp", "ctx", None),
        P(),
        P(),
    )
    return jax.shard_map(
        per_device,
        mesh=mesh,
        in_specs=placed,
        out_specs=(
            P("dp", "ctx", None),
            P("dp", "ctx", None),
            P("dp", "ctx", None),
            P("dp", "ctx", None),
            P(),
        ),
        check_vma=False,
    )
```

profile of v0, /device:TPU:0, one launch (start us, length us, event | category | flops | bytes accessed | tf_op | source)
XLA Modules:
  0.0 354.4 jit_solution(14615889557479074196)
XLA Ops:
  12.8 3.3 collective-permute-start
  16.7 4.5 %collective-permute-start.1 = (bf16[512,1024]{0,1:T(8,128)(2,1)S(1)}, bf16[512,1024]{0,1:T(8,128)(2,1)}, u32[]{:S(2)}, u32[]{:S(2)}) collective-permute-start(bf16[512,1024]{0,1:T(8,128)(2,1)S(1)} %bitcast.242), channel_id=1, source_target_pairs={{0,1},{1,2},{2,3},{3,4},{4,5},{5,6},{6,7},{8,9},{9,10},{10,11},{11... | collective-permute-start | bytes 3145736 | tf_op jit(solution)/shard_map/ppermute | solution.py:17
  22.7 2.3 copy.26
  25.1 2.9 maximum_bitcast_fusion
  28.0 2.9 maximum_bitcast_fusion.1
  30.9 7.3 %all-gather.7.cloned.1.call-done = bf16[1,512,1024]{2,1,0:T(8,128)(2,1)} async-done(((bf16[1,64,1024]{2,1,0:T(8,128)(2,1)}), bf16[1,512,1024]{2,1,0:T(8,128)(2,1)}) %all-gather.7.cloned.1.call-update) | async-done | bytes 1048592 | tf_op jit(solution)/shard_map/all_gather | solution.py:96
  38.2 25.5 %all-gather.5.cloned.1.call-done = bf16[1,512,1024]{2,1,0:T(8,128)(2,1)} async-done(((bf16[1,64,1024]{2,1,0:T(8,128)(2,1)}), bf16[1,512,1024]{2,1,0:T(8,128)(2,1)}) %all-gather.5.cloned.1.call-update) | async-done | bytes 1048592 | tf_op jit(solution)/shard_map/all_gather | solution.py:95
  65.4 169.8 %while.29 = (s32[]{:T(128)}, bf16[8,512,128]{1,2,0:T(8,128)(2,1)}, bf16[8,512,128]{2,1,0:T(8,128)(2,1)}, f32[8,1024,128]{2,1,0:T(8,128)}, f32[8,1024,128]{2,1,0:...) while((s32[]{:T(128)}, bf16[8,512,128]{1,2,0:T(8,128)(2,1)}, ...), condition=%wide.region_8.9_spmd.clone, body=%wide.region_0.8_spmd.clone.sunk | while | flops 869654016 | bytes 19551504 | solution.py:125
  77.8 2.5 select_reduce_fusion.2
  99.0 2.5 select_reduce_fusion.2
  109.8 2.0 fusion.160
  120.2 2.5 select_reduce_fusion.2
  141.4 2.5 select_reduce_fusion.2
  162.7 2.5 select_reduce_fusion.2
  183.9 2.5 select_reduce_fusion.2
  205.1 2.5 select_reduce_fusion.2
  215.9 2.0 fusion.160
  226.4 2.5 select_reduce_fusion.2
  235.3 4.0 %slice_bitcast_fusion.3 = (f32[8,64,8,128]{3,2,1,0:T(8,128)}, f32[8,64,8,128]{3,2,1,0:T(8,128)S(1)}) fusion(f32[1024,8,128]{2,0,1:T(8,128)} %bitcast.240), kind=kLoop, calls=%fused_computation.130 | loop fusion | bytes 8388608
  248.4 79.4 %psum.23 = f32[8]{0:T(128)} all-reduce(f32[8]{0:T(128)S(1)} %get-tuple-element.149), channel_id=1, replica_groups=mesh['dp'=4,'ctx'=8] {'dp','ctx'}, use_global_device_ids=true, to_apply=%region_11.12 | all-reduce | flops 8 | bytes 64 | tf_op jit(solution)/shard_map/psum | solution.py:152
  331.1 4.3 %all-reduce.3.cloned.1.call-done = (f32[64,1024]{1,0:T(8,128)}, f32[64,1024]{1,0:T(8,128)}) async-done(((f32[64,1024]{1,0:T(8,128)}, f32[64,1024]{1,0:T(8,128)}), (f32[64,1024]{1,0:T(8,128)}, f32[64,1024]{1,0:T(8,128)})) %all-reduce.3.cloned.1.call-update) | async-done | bytes 524304 | tf_op jit(solution)/shard_map/psum | solution.py:147
  335.3 3.8 %gather_fusion = f32[512,1024]{1,0:T(8,128)S(1)} fusion(f32[64,1024]{1,0:T(8,128)} %get-tuple-element.315, s32[1024]{0:T(1024)S(1)} %pad_clamp_fusion), kind=kCustom, calls=%fused_computation | custom fusion | bytes 4196352 | tf_op jit(solution)/shard_map/gather | solution.py:150
  339.2 2.7 gather_fusion.1
  341.8 6.0 %fusion.99 = (bf16[1,512,1024]{2,1,0:T(8,128)(2,1)}, bf16[1,512,1024]{2,1,0:T(8,128)(2,1)}) fusion(f32[512,1024]{1,0:T(8,128)} %gather_fusion.1, f32[512,1024]{1,0:T(8,128)} %collective-permute-done.3, f32[8,64,8,128]{3,2,1,0:T(8,128)} %get-tuple-element.327, pred[512]{0:T(512)(128)(4,1)S(1)} %fusion.108, f32[512,1024]{1,0:T(8,128)S(1)} %gather_fusion, ...), kind=kLoop, calls=%fused_computation.134 | loop fusion | flops 4194304 | bytes 14680576 | tf_op jit(solution)/shard_map/convert_element_type | solution.py:157
  (220 shorter events, 157.1 us)
Async XLA Ops:
  7.2 9.0 %copy-start.3 = (bf16[1,512,1024]{2,1,0:T(8,128)(2,1)S(1)}, bf16[1,512,1024]{2,1,0:T(8,128)(2,1)}, u32[]{:S(2)}) copy-start(bf16[1,512,1024]{2,1,0:T(8,128)(2,1)} %param.18) | copy-start | bytes 3145732
  7.2 31.1 %all-gather.7.cloned.1.call-start = ((), (), s32[]{:S(2)}) async-start(), calls=%async_computation.1 | async-start | bytes 1179648 | tf_op jit(solution)/shard_map/all_gather | solution.py:96
  9.6 54.1 %all-gather.5.cloned.1.call-start = ((), (), s32[]{:S(2)}) async-start(), calls=%async_computation | async-start | bytes 1179648 | tf_op jit(solution)/shard_map/all_gather | solution.py:95
  11.2 324.1 %all-reduce.3.cloned.1.call-start = ((), (), s32[]{:S(2)}) async-start(), calls=%async_computation.2 | async-start | bytes 1048576 | tf_op jit(solution)/shard_map/psum | solution.py:147
  12.8 12.3 %collective-permute-start = (bf16[512,1024]{0,1:T(8,128)(2,1)S(1)}, bf16[512,1024]{0,1:T(8,128)(2,1)}, u32[]{:S(2)}, u32[]{:S(2)}) collective-permute-start(bf16[512,1024]{0,1:T(8,128)(2,1)S(1)} %bitcast.244), channel_id=1, source_target_pairs={{0,1},{1,2},{2,3},{3,4},{4,5},{5,6},{6,7},{8,9},{9,10},{10,11},{11... | collective-permute-start | bytes 3145736 | tf_op jit(solution)/shard_map/ppermute | solution.py:17
  16.7 11.3 %collective-permute-start.1 = (bf16[512,1024]{0,1:T(8,128)(2,1)S(1)}, bf16[512,1024]{0,1:T(8,128)(2,1)}, u32[]{:S(2)}, u32[]{:S(2)}) collective-permute-start(bf16[512,1024]{0,1:T(8,128)(2,1)S(1)} %bitcast.242), channel_id=1, source_target_pairs={{0,1},{1,2},{2,3},{3,4},{4,5},{5,6},{6,7},{8,9},{9,10},{10,11},{11... | collective-permute-start | bytes 3145736 | tf_op jit(solution)/shard_map/ppermute | solution.py:17
  28.0 37.5 %copy-start.2 = (bf16[1,512,1024]{1,2,0:T(8,128)(2,1)S(1)}, bf16[1,512,1024]{1,2,0:T(8,128)(2,1)}, u32[]{:S(2)}) copy-start(bf16[1,512,1024]{1,2,0:T(8,128)(2,1)} %copy.26) | copy-start | bytes 3145732
  28.0 37.5 %copy-start.8 = (f32[8]{0:T(128)S(1)}, f32[8]{0:T(128)}, u32[]{:S(2)}) copy-start(f32[8]{0:T(128)} %param.20) | copy-start | bytes 100
  239.2 3.0 copy-start.1
  240.8 101.0 %collective-permute-start.2 = (f32[512,1024]{1,0:T(8,128)}, f32[512,1024]{1,0:T(8,128)}, u32[]{:S(2)}, u32[]{:S(2)}) collective-permute-start(f32[512,1024]{1,0:T(8,128)} %bitcast.178), channel_id=1, source_target_pairs={{1,0},{2,1},{3,2},{4,3},{5,4},{6,5},{7,6},{9,8},{10,9},{11,10},{12... | collective-permute-start | bytes 6291464 | tf_op jit(solution)/shard_map/ppermute | solution.py:17
  243.9 2.9 copy-start.7
  243.9 3.7 %copy-start.6 = (f32[8,64,128]{2,1,0:T(8,128)S(1)}, f32[8,64,128]{2,1,0:T(8,128)}, u32[]{:S(2)}) copy-start(f32[8,64,128]{2,1,0:T(8,128)} %get-tuple-element.146) | copy-start | bytes 786436
  243.9 83.9 %copy-start.5 = (bf16[8,512,128]{2,1,0:T(8,128)(2,1)S(1)}, bf16[8,512,128]{2,1,0:T(8,128)(2,1)}, u32[]{:S(2)}) copy-start(bf16[8,512,128]{2,1,0:T(8,128)(2,1)} %get-tuple-element.144) | copy-start | bytes 3145732
  245.5 96.3 %collective-permute-start.3 = (f32[512,1024]{1,0:T(8,128)}, f32[512,1024]{1,0:T(8,128)}, u32[]{:S(2)}, u32[]{:S(2)}) collective-permute-start(f32[512,1024]{1,0:T(8,128)} %bitcast.177), channel_id=1, source_target_pairs={{1,0},{2,1},{3,2},{4,3},{5,4},{6,5},{7,6},{9,8},{10,9},{11,10},{12... | collective-permute-start | bytes 6291464 | tf_op jit(solution)/shard_map/ppermute | solution.py:17
  327.8 2.0 copy-start.4
  335.3 3.8 %copy-start = (f32[64,1024]{1,0:T(8,128)S(1)}, f32[64,1024]{1,0:T(8,128)}, u32[]{:S(2)}) copy-start(f32[64,1024]{1,0:T(8,128)} %get-tuple-element.316) | copy-start | bytes 786436
Sparse Core Ops, SparseCore 0:
  9.9 28.2 all-gather.6
  40.1 23.5 all-gather.4
  248.4 86.8 all-reduce.2
where the time goes:
time: 357 us; the launch traced here: 354 us
  matrix products  133 us (37%)
  blocking collectives  79.4 us (22%)
  waiting for transfers between devices  37.1 us (10%)
  local copies, waits for them, and re-layouts  36.4 us (10%)
  other arithmetic  32.7 us (9%)
  between operations  14.7 us (4%)
  starting transfers between devices  10.7 us (3%)
  loops' own time  10 us (3%)
    psum x1, blocking collectives, per_device(): bias_grad = lax.psum(dbias, ('dp', 'ctx'))  79.4 us
    all_gather x1, waiting for transfers between devices, per_device(): lax.all_gather(piece_k, 'ctx', axis=0, tiled=True)  25.5 us
    dot_general x8, matrix products, head_block(): jnp.dot(doh, vb.T, preferred_element_type=jnp.float32) - delta[:, None]  19.7 us
    dot_general x8, matrix products, head_block(): jnp.dot(qh, kb.T, preferred_element_type=jnp.float32) * scale  15.9 us
    unnamed x29, local copies, waits for them, and re-layouts  13.2 us
    dot_general x8, matrix products, head_block(): jnp.dot(wb16, vb, preferred_element_type=jnp.float32)  12.9 us
    dot_general x8, matrix products, head_block(): jnp.dot(wc16, vc, preferred_element_type=jnp.float32)  12.9 us
    dot_general x8, matrix products, head_block(): dvb = jnp.dot(wb16.T, doh, preferred_element_type=jnp.float32)  12.7 us
  transfers between devices with their start and end apart: 7, of which 3 were waited for; matrix products, arithmetic and copies ran while one was open for 8% of the time, Pallas kernels for 0%

commit v1 on v0

--- a/solution.py
+++ b/solution.py
@@ -149,7 +149,7 @@
     source = jnp.clip(qpos // STRIDE * CB + qpos % CB, 0, ncol * CB - 1)
     own_dk = own_dk + jnp.where(flags[:, None], summed_k[source], 0.0)
     own_dv = own_dv + jnp.where(flags[:, None], summed_v[source], 0.0)
-    bias_grad = lax.psum(dbias, ("dp", "ctx"))
+    bias_grad = jnp.sum(lax.all_gather(dbias, ("dp", "ctx")), axis=0)
     return (
         attended[None],
         query_grad[None],

time: 357 us -> 359 us (level)
    psum x1 -> x0, blocking collectives: 79.4 us -> none  [per_device(): bias_grad = lax.psum(dbias, ('dp', 'ctx'))]
    unnamed x0 -> x1, blocking collectives: none -> 75.9 us
    unnamed x29 -> x31, local copies, waits for them, and re-layouts: 13.2 us -> 13.3 us
where the time goes in v1:
time: 359 us; the launch traced here: 356 us
  matrix products  134 us (37%)
  blocking collectives  75.9 us (21%)
  waiting for transfers between devices  39.9 us (11%)
  local copies, waits for them, and re-layouts  36.6 us (10%)
  other arithmetic  33.2 us (9%)
  between operations  14.7 us (4%)
  loops' own time  11 us (3%)
  starting transfers between devices  10.7 us (3%)
    unnamed x1, blocking collectives  75.9 us
    all_gather x1, waiting for transfers between devices, per_device(): lax.all_gather(piece_k, 'ctx', axis=0, tiled=True)  25.5 us
    dot_general x8, matrix products, head_block(): jnp.dot(doh, vb.T, preferred_element_type=jnp.float32) - delta[:, None]  19.7 us
    dot_general x8, matrix products, head_block(): jnp.dot(qh, kb.T, preferred_element_type=jnp.float32) * scale  15.9 us
    unnamed x31, local copies, waits for them, and re-layouts  13.3 us
    dot_general x8, matrix products, head_block(): jnp.dot(wb16, vb, preferred_element_type=jnp.float32)  12.9 us
    dot_general x8, matrix products, head_block(): jnp.dot(wc16, vc, preferred_element_type=jnp.float32)  12.9 us
    dot_general x8, matrix products, head_block(): dvb = jnp.dot(wb16.T, doh, preferred_element_type=jnp.float32)  12.7 us
  transfers between devices with their start and end apart: 7, of which 3 were waited for; matrix products, arithmetic and copies ran while one was open for 8% of the time, Pallas kernels for 0%

profile of v1, /device:TPU:0, one launch (start us, length us, event | category | flops | bytes accessed | tf_op | source)
XLA Modules:
  0.0 356.0 jit_solution(3540969112089438092)
XLA Ops:
  12.8 3.3 collective-permute-start
  16.7 4.6 %collective-permute-start.1 = (bf16[512,1024]{0,1:T(8,128)(2,1)S(1)}, bf16[512,1024]{0,1:T(8,128)(2,1)}, u32[]{:S(2)}, u32[]{:S(2)}) collective-permute-start(bf16[512,1024]{0,1:T(8,128)(2,1)S(1)} %bitcast.242), channel_id=1, source_target_pairs={{0,1},{1,2},{2,3},{3,4},{4,5},{5,6},{6,7},{8,9},{9,10},{10,11},{11... | collective-permute-start | bytes 3145736 | tf_op jit(solution)/shard_map/ppermute | solution.py:17
  22.7 2.3 copy.26
  25.1 2.9 maximum_bitcast_fusion
  28.0 2.9 maximum_bitcast_fusion.1
  30.9 7.4 %all-gather.8.cloned.1.call-done = bf16[1,512,1024]{2,1,0:T(8,128)(2,1)} async-done(((bf16[1,64,1024]{2,1,0:T(8,128)(2,1)}), bf16[1,512,1024]{2,1,0:T(8,128)(2,1)}) %all-gather.8.cloned.1.call-update) | async-done | bytes 1048592 | tf_op jit(solution)/shard_map/all_gather | solution.py:96
  38.2 25.5 %all-gather.6.cloned.1.call-done = bf16[1,512,1024]{2,1,0:T(8,128)(2,1)} async-done(((bf16[1,64,1024]{2,1,0:T(8,128)(2,1)}), bf16[1,512,1024]{2,1,0:T(8,128)(2,1)}) %all-gather.6.cloned.1.call-update) | async-done | bytes 1048592 | tf_op jit(solution)/shard_map/all_gather | solution.py:95
  65.4 171.3 %while.29 = (s32[]{:T(128)}, bf16[8,512,128]{1,2,0:T(8,128)(2,1)}, bf16[8,512,128]{2,1,0:T(8,128)(2,1)}, f32[8,1024,128]{2,1,0:T(8,128)}, f32[8,1024,128]{2,1,0:...) while((s32[]{:T(128)}, bf16[8,512,128]{1,2,0:T(8,128)(2,1)}, ...), condition=%wide.region_8.9_spmd.clone, body=%wide.region_0.8_spmd.clone.sunk | while | flops 869654016 | bytes 19551504 | solution.py:125
  77.8 2.5 select_reduce_fusion.2
  99.3 2.5 select_reduce_fusion.2
  110.2 2.0 fusion.160
  120.7 2.5 select_reduce_fusion.2
  142.1 2.5 select_reduce_fusion.2
  153.0 2.0 fusion.160
  163.5 2.5 select_reduce_fusion.2
  184.9 2.5 select_reduce_fusion.2
  206.3 2.5 select_reduce_fusion.2
  227.8 2.5 select_reduce_fusion.2
  236.8 4.0 %slice_bitcast_fusion.3 = (f32[8,64,8,128]{3,2,1,0:T(8,128)}, f32[8,64,8,128]{3,2,1,0:T(8,128)S(1)}) fusion(f32[1024,8,128]{2,0,1:T(8,128)} %bitcast.240), kind=kLoop, calls=%fused_computation.130 | loop fusion | bytes 8388608
  253.4 75.9 %all-reduce = f32[256]{0:T(256)S(1)} all-reduce(f32[256]{0:T(256)S(1)} %dynamic-update-slice.6), channel_id=4, replica_groups=mesh['dp'=4,'ctx'=8] {'dp','ctx'}, use_global_device_ids=true, to_apply=%add | all-reduce | flops 256 | bytes 2048
  330.0 7.0 %all-reduce.4.cloned.1.call-done = (f32[64,1024]{1,0:T(8,128)}, f32[64,1024]{1,0:T(8,128)}) async-done(((f32[64,1024]{1,0:T(8,128)}, f32[64,1024]{1,0:T(8,128)}), (f32[64,1024]{1,0:T(8,128)}, f32[64,1024]{1,0:T(8,128)})) %all-reduce.4.cloned.1.call-update) | async-done | bytes 524304 | tf_op jit(solution)/shard_map/psum | solution.py:147
  337.0 3.8 %gather_fusion = f32[512,1024]{1,0:T(8,128)S(1)} fusion(f32[64,1024]{1,0:T(8,128)} %get-tuple-element.315, s32[1024]{0:T(1024)S(1)} %pad_clamp_fusion), kind=kCustom, calls=%fused_computation | custom fusion | bytes 4196352 | tf_op jit(solution)/shard_map/gather | solution.py:150
  340.8 2.7 gather_fusion.1
  343.5 6.0 %fusion.99 = (bf16[1,512,1024]{2,1,0:T(8,128)(2,1)}, bf16[1,512,1024]{2,1,0:T(8,128)(2,1)}) fusion(f32[512,1024]{1,0:T(8,128)} %gather_fusion.1, f32[512,1024]{1,0:T(8,128)} %collective-permute-done.3, f32[8,64,8,128]{3,2,1,0:T(8,128)} %get-tuple-element.327, pred[512]{0:T(512)(128)(4,1)S(1)} %fusion.108, f32[512,1024]{1,0:T(8,128)S(1)} %gather_fusion, ...), kind=kLoop, calls=%fused_computation.134 | loop fusion | flops 4194304 | bytes 14680576 | tf_op jit(solution)/shard_map/convert_element_type | solution.py:157
  (224 shorter events, 158.5 us)
Async XLA Ops:
  7.2 9.0 %copy-start.3 = (bf16[1,512,1024]{2,1,0:T(8,128)(2,1)S(1)}, bf16[1,512,1024]{2,1,0:T(8,128)(2,1)}, u32[]{:S(2)}) copy-start(bf16[1,512,1024]{2,1,0:T(8,128)(2,1)} %param.18) | copy-start | bytes 3145732
  7.2 31.1 %all-gather.8.cloned.1.call-start = ((), (), s32[]{:S(2)}) async-start(), calls=%async_computation.1 | async-start | bytes 1179648 | tf_op jit(solution)/shard_map/all_gather | solution.py:96
  9.6 54.1 %all-gather.6.cloned.1.call-start = ((), (), s32[]{:S(2)}) async-start(), calls=%async_computation | async-start | bytes 1179648 | tf_op jit(solution)/shard_map/all_gather | solution.py:95
  11.2 325.8 %all-reduce.4.cloned.1.call-start = ((), (), s32[]{:S(2)}) async-start(), calls=%async_computation.2 | async-start | bytes 1048576 | tf_op jit(solution)/shard_map/psum | solution.py:147
  12.8 12.3 %collective-permute-start = (bf16[512,1024]{0,1:T(8,128)(2,1)S(1)}, bf16[512,1024]{0,1:T(8,128)(2,1)}, u32[]{:S(2)}, u32[]{:S(2)}) collective-permute-start(bf16[512,1024]{0,1:T(8,128)(2,1)S(1)} %bitcast.244), channel_id=1, source_target_pairs={{0,1},{1,2},{2,3},{3,4},{4,5},{5,6},{6,7},{8,9},{9,10},{10,11},{11... | collective-permute-start | bytes 3145736 | tf_op jit(solution)/shard_map/ppermute | solution.py:17
  16.7 11.3 %collective-permute-start.1 = (bf16[512,1024]{0,1:T(8,128)(2,1)S(1)}, bf16[512,1024]{0,1:T(8,128)(2,1)}, u32[]{:S(2)}, u32[]{:S(2)}) collective-permute-start(bf16[512,1024]{0,1:T(8,128)(2,1)S(1)} %bitcast.242), channel_id=1, source_target_pairs={{0,1},{1,2},{2,3},{3,4},{4,5},{5,6},{6,7},{8,9},{9,10},{10,11},{11... | collective-permute-start | bytes 3145736 | tf_op jit(solution)/shard_map/ppermute | solution.py:17
  27.9 37.5 %copy-start.2 = (bf16[1,512,1024]{1,2,0:T(8,128)(2,1)S(1)}, bf16[1,512,1024]{1,2,0:T(8,128)(2,1)}, u32[]{:S(2)}) copy-start(bf16[1,512,1024]{1,2,0:T(8,128)(2,1)} %copy.26) | copy-start | bytes 3145732
  28.0 37.5 %copy-start.8 = (f32[8]{0:T(128)S(1)}, f32[8]{0:T(128)}, u32[]{:S(2)}) copy-start(f32[8]{0:T(128)} %param.20) | copy-start | bytes 100
  240.7 3.0 copy-start.1
  242.3 101.2 %collective-permute-start.2 = (f32[512,1024]{1,0:T(8,128)}, f32[512,1024]{1,0:T(8,128)}, u32[]{:S(2)}, u32[]{:S(2)}) collective-permute-start(f32[512,1024]{1,0:T(8,128)} %bitcast.178), channel_id=1, source_target_pairs={{1,0},{2,1},{3,2},{4,3},{5,4},{6,5},{7,6},{9,8},{10,9},{11,10},{12... | collective-permute-start | bytes 6291464 | tf_op jit(solution)/shard_map/ppermute | solution.py:17
  245.4 2.9 copy-start.7
  245.4 3.7 %copy-start.6 = (f32[8,64,128]{2,1,0:T(8,128)S(1)}, f32[8,64,128]{2,1,0:T(8,128)}, u32[]{:S(2)}) copy-start(f32[8,64,128]{2,1,0:T(8,128)} %get-tuple-element.146) | copy-start | bytes 786436
  245.4 4.5 %copy-start.5 = (bf16[8,512,128]{2,1,0:T(8,128)(2,1)S(1)}, bf16[8,512,128]{2,1,0:T(8,128)(2,1)}, u32[]{:S(2)}) copy-start(bf16[8,512,128]{2,1,0:T(8,128)(2,1)} %get-tuple-element.144) | copy-start | bytes 3145732
  247.0 96.5 %collective-permute-start.3 = (f32[512,1024]{1,0:T(8,128)}, f32[512,1024]{1,0:T(8,128)}, u32[]{:S(2)}, u32[]{:S(2)}) collective-permute-start(f32[512,1024]{1,0:T(8,128)} %bitcast.177), channel_id=1, source_target_pairs={{1,0},{2,1},{3,2},{4,3},{5,4},{6,5},{7,6},{9,8},{10,9},{11,10},{12... | collective-permute-start | bytes 6291464 | tf_op jit(solution)/shard_map/ppermute | solution.py:17
  249.9 2.0 copy-start.4
  337.0 3.8 %copy-start = (f32[64,1024]{1,0:T(8,128)S(1)}, f32[64,1024]{1,0:T(8,128)}, u32[]{:S(2)}) copy-start(f32[64,1024]{1,0:T(8,128)} %get-tuple-element.316) | copy-start | bytes 786436
Sparse Core Ops, SparseCore 0:
  9.9 28.2 all-gather.7
  40.1 23.5 all-gather.5
  250.0 86.9 all-reduce.3
